TPU v7x, 32 devices: a whole 2x2x4 slice. The times are simulated.
32 devices in a mesh: region: 16 (over z, y, core), panel: 2 (over x).
Axes of the slice: x: 2, y: 2, z: 4, core: 2. Of those that a mesh axis runs over, the one named last changes fastest.
Arguments:
- multipliers: bfloat16 [16, 4096, 512], P('region', 'panel'), may hold values from -6 to 6
- flexibility: bfloat16 [16, 4096, 4096], P('region', 'panel'), as said below
- interface_sizes: int32 [16], P('region'), may hold values from 1024 to 4096, as said below
- send_rows: int32 [16, 2, 1536], replicated, may hold values from 0 to 4095, as said below
- recv_rows: int32 [16, 2, 1536], P('region'), may hold values from 0 to 4095, as said below
- recv_pos: int32 [16, 2, 1536], P('region'), may hold values from 0 to 1534
- recv_weight: float32 [16, 2, 1536], P('region'), may hold values from 0 to 1
Outputs:
- dual_image: float32 [16, 4096, 512], P('region', None, 'panel')
Inputs may be any that keep to these rules, and one draw needn't show every extreme that they name: `flexibility`: each region's matrix is symmetric. `interface_sizes`: A multiple of 128. `send_rows`: every entry of region r is below interface_sizes[r]; side 0 faces region r - 1 and side 1 region r + 1 around the loop; rows may repeat. `recv_rows`: every entry of region r is below interface_sizes[r]; rows may repeat.
All inputs are finite; a program needn't handle non-finite values.
Results may differ from a plain program's by a relative error of at most 0.0029.
Values may be sent and summed in bfloat16 or wider, within the bound.
No kernel may reach another device: no remote copies, remote signals or barrier semaphores. Data moves between devices by JAX's collectives and lax.ppermute only.
A program may use at most 128 MiB of HBM per device.

v0:
```python
import jax
import jax.numpy as jnp
from jax import lax
from jax.sharding import PartitionSpec as P


def shifted(value, axis, steps):
    count = lax.axis_size(axis)
    pairs = [(source, (source + steps) % count) for source in range(count)]
    return lax.ppermute(value, axis, pairs)


def interpolate(arrived, position, weight):
    first_rows = arrived[position].astype(jnp.float32)
    second_rows = arrived[position + 1].astype(jnp.float32)
    return (1.0 - weight)[:, None] * first_rows + weight[:, None] * second_rows


def on_device(
    multipliers, flexibility, interface_sizes, send_rows, recv_rows, recv_pos, recv_weight
):
    local_block = multipliers[0]
    flex_panel = flexibility[0]
    rows_here = local_block.shape[0]
    first_row = lax.axis_index("panel") * rows_here
    row_ids = first_row + jnp.arange(rows_here, dtype=jnp.int32)
    live_here = (row_ids < interface_sizes[0])[:, None]
    live_block = jnp.where(live_here, local_block, jnp.zeros((), local_block.dtype))
    image = jnp.dot(
        flex_panel,
        lax.all_gather(live_block, "panel", axis=0, tiled=True),
        preferred_element_type=jnp.float32,
    )
    settled = jnp.where(live_here, image, jnp.zeros((), image.dtype)).astype(jnp.bfloat16)
    columns_all = lax.all_to_all(settled, "panel", split_axis=1, concat_axis=0, tiled=True)
    region_index = lax.axis_index("region")
    regions = lax.axis_size("region")
    lower_region = (region_index + regions - 1) % regions
    upper_region = (region_index + 1) % regions
    lower_all = shifted(columns_all, "region", 1)
    upper_all = shifted(columns_all, "region", -1)
    from_lower = lower_all[send_rows[lower_region, 1]]
    from_upper = upper_all[send_rows[upper_region, 0]]
    jump_lower = interpolate(from_lower, recv_pos[0, 0], recv_weight[0, 0])
    jump_upper = interpolate(from_upper, recv_pos[0, 1], recv_weight[0, 1])
    jumps = jnp.concatenate([jump_lower, jump_upper], axis=0)
    targets = recv_rows[0].reshape(-1)
    result = columns_all.astype(jnp.float32).at[targets].add(-jumps)
    return result[None]


def solution(mesh):
    in_specs = (
        P("region", "panel", None),
        P("region", "panel", None),
        P("region"),
        P(),
        P("region", None, None),
        P("region", None, None),
        P("region", None, None),
    )
    out_specs = P("region", None, "panel")
    return jax.shard_map(
        on_device, mesh=mesh, in_specs=in_specs, out_specs=out_specs, check_vma=False
    )
```

profile of v0, /device:TPU:1, one launch (start us, length us, event | category | flops | bytes accessed | tf_op | source)
XLA Modules:
  0.0 225.4 jit_solution(8095538490072219212)
XLA Ops:
  6.5 0.0 all-gather.2.cloned.1.call-start
  7.2 2.8 %bitcast_select_fusion = bf16[2048,512]{1,0:T(8,128)(2,1)} fusion(bf16[1,2048,512]{2,1,0:T(8,128)(2,1)} %param.7, pred[2048]{0:T(1024)(128)(4,1)S(1)} %add_compare_fusion), kind=kLoop, calls=%fused_computation.14 | loop fusion | flops 1048576 | bytes 4196352 | tf_op jit(solution)/shard_map/jit(_where)/select_n | solution.py:28
  10.0 0.0 all-gather.2.cloned.1.call-update
  10.0 58.8 %all-gather.2.cloned.1.call-done = bf16[4096,512]{1,0:T(8,128)(2,1)} async-done(((bf16[2048,512]{1,0:T(8,128)(2,1)}), bf16[4096,512]{1,0:T(8,128)(2,1)}) %all-gather.2.cloned.1.call-update) | async-done | bytes 4194320 | tf_op jit(solution)/shard_map/all_gather | solution.py:31
  68.8 14.7 %select_convert_fusion = bf16[512,2048]{1,0:T(8,128)(2,1)} fusion(bf16[4096,512]{1,0:T(8,128)(2,1)} %all-gather.2.cloned.1.call-done, bf16[1,2048,4096]{2,1,0:T(8,128)(2,1)} %param.8, pred[2048]{0:T(1024)(128)(4,1)S(1)} %add_compare_fusion), kind=kOutput, calls=%fused_computation.9 | convolution fusion | flops 8592031744 | bytes 23070720 | tf_op jit(solution)/shard_map/dot_general | solution.py:29
  83.4 3.9 %all-to-all-start = ((bf16[2048,2,256]{0,2,1:T(8,128)(2,1)}), bf16[2048,2,256]{0,2,1:T(8,128)(2,1)S(1)}, u32[]{:S(2)}, u32[]{:S(2)}) async-start(bf16[2048,2,256]{0,2,1:T(8,128)(2,1)} %bitcast.42), calls=%async_computation | async-start | bytes 4194304 | tf_op jit(solution)/shard_map/all_to_all | solution.py:35
  87.4 0.8 fusion.7
  88.2 0.1 fusion.8
  88.3 23.1 %all-to-all-done = bf16[2048,2,256]{0,2,1:T(8,128)(2,1)S(1)} async-done(((bf16[2048,2,256]{0,2,1:T(8,128)(2,1)}), bf16[2048,2,256]{0,2,1:T(8,128)(2,1)S(1)}, u32[]{:S(2)}, u32[]{:S(2)}) %all-to-all-start) | async-done | bytes 2097184 | tf_op jit(solution)/shard_map/all_to_all | solution.py:35
  111.4 2.5 %copy.9 = bf16[2,2048,256]{2,1,0:T(8,128)(2,1)} copy(bf16[2,2048,256]{1,2,0:T(8,128)(2,1)S(1)} %bitcast.41) | data formatting | bytes 4194304 | tf_op jit(solution)/shard_map/all_to_all | solution.py:35
  113.9 2.8 %collective-permute-start = (bf16[4096,256]{1,0:T(8,128)(2,1)}, bf16[4096,256]{1,0:T(8,128)(2,1)}, u32[]{:S(2)}, u32[]{:S(2)}) collective-permute-start(bf16[4096,256]{1,0:T(8,128)(2,1)} %bitcast.6), channel_id=1, source_target_pairs={{0,2},{2,4},{4,6},{6,8},{8,10},{10,12},{12,14},{14,16},{16,18},{18... | collective-permute-start | bytes 6291464 | tf_op jit(solution)/shard_map/ppermute | solution.py:10
  116.7 0.0 collective-permute-start.1
  116.8 3.9 %bitcast_convert_fusion = f32[4096,256]{1,0:T(8,128)} fusion(bf16[2,2048,256]{2,1,0:T(8,128)(2,1)} %copy.9), kind=kLoop, calls=%fused_computation.45 | loop fusion | flops 1048576 | bytes 6291456 | tf_op jit(solution)/shard_map/convert_element_type | solution.py:48
  120.7 41.7 %collective-permute-done = bf16[4096,256]{1,0:T(8,128)(2,1)} collective-permute-done((bf16[4096,256]{1,0:T(8,128)(2,1)}, bf16[4096,256]{1,0:T(8,128)(2,1)}, u32[]{:S(2)}, u32[]{:S(2)}) %collective-permute-start) | collective-permute-done | bytes 2097184 | tf_op jit(solution)/shard_map/ppermute | solution.py:10
  162.4 5.5 %gather_fusion = bf16[1536,256]{1,0:T(8,128)(2,1)S(1)} fusion(bf16[4096,256]{1,0:T(8,128)(2,1)} %collective-permute-done, s32[2048]{0:T(1024)S(1)} %pad_clamp_fusion.5), kind=kCustom, calls=%fused_computation | custom fusion | bytes 1579008 | tf_op jit(solution)/shard_map/gather | solution.py:42
  168.0 5.4 %gather_fusion.1 = bf16[1536,256]{1,0:T(8,128)(2,1)} fusion(bf16[1536,256]{1,0:T(8,128)(2,1)S(1)} %gather_fusion, s32[2048]{0:T(1024)S(1)} %get-tuple-element.16), kind=kCustom, calls=%fused_computation.1 | custom fusion | bytes 1579008 | tf_op jit(solution)/shard_map/gather | solution.py:14
  173.3 5.4 %gather_fusion.2 = bf16[1536,256]{1,0:T(8,128)(2,1)} fusion(bf16[1536,256]{1,0:T(8,128)(2,1)S(1)} %gather_fusion, s32[2048]{0:T(1024)S(1)} %get-tuple-element.15), kind=kCustom, calls=%fused_computation.2 | custom fusion | bytes 1579008 | tf_op jit(solution)/shard_map/gather | solution.py:15
  178.7 0.0 collective-permute-done.1
  178.7 4.8 %gather_fusion.3 = bf16[1536,256]{1,0:T(8,128)(2,1)S(1)} fusion(bf16[4096,256]{1,0:T(8,128)(2,1)S(1)} %collective-permute-done.1, s32[2048]{0:T(1024)S(1)} %pad_clamp_fusion.2), kind=kCustom, calls=%fused_computation.3 | custom fusion | bytes 1579008 | tf_op jit(solution)/shard_map/gather | solution.py:43
  183.4 5.4 %gather_fusion.4 = bf16[1536,256]{1,0:T(8,128)(2,1)} fusion(bf16[1536,256]{1,0:T(8,128)(2,1)S(1)} %gather_fusion.3, s32[2048]{0:T(1024)S(1)} %get-tuple-element.14), kind=kCustom, calls=%fused_computation.4 | custom fusion | bytes 1579008 | tf_op jit(solution)/shard_map/gather | solution.py:14
  188.8 5.3 %gather_fusion.5 = bf16[1536,256]{1,0:T(8,128)(2,1)} fusion(bf16[1536,256]{1,0:T(8,128)(2,1)S(1)} %gather_fusion.3, s32[2048]{0:T(1024)S(1)} %get-tuple-element.13), kind=kCustom, calls=%fused_computation.5 | custom fusion | bytes 1579008 | tf_op jit(solution)/shard_map/gather | solution.py:15
  194.1 2.0 multiply_add_fusion.1
  196.1 0.5 multiply_add_fusion
  196.6 22.0 %scatter_custom_fusion = f32[4096,256]{1,0:T(8,128)} fusion(f32[4096,256]{1,0:T(8,128)} %bitcast_convert_fusion, s32[3072]{0:T(1024)S(1)} %bitcast.45, f32[1536,256]{1,0:T(8,128)S(1)} %multiply_add_fusion, f32[]{:T(128)} %constant.63, f32[1536,256]{1,0:T(8,128)S(1)} %multiply_add_fusion.1), kind=kCustom, calls=%fused_computation.11 | custom fusion | flops 2359296 | bytes 7340544 | tf_op jit(solution)/shard_map/scatter-add | solution.py:48
  (19 shorter events, 0.1 us)
Async XLA Ops:
  6.5 62.2 %all-gather.2.cloned.1.call-start = ((), (), s32[]{:S(2)}) async-start(), calls=%async_computation.1 | async-start | bytes 6291456 | tf_op jit(solution)/shard_map/all_gather | solution.py:31
  83.4 4.7 %copy-start.4 = (s32[1,2,1536]{2,1,0:T(2,128)S(1)}, s32[1,2,1536]{2,1,0:T(2,128)}, u32[]{:S(2)}) copy-start(s32[1,2,1536]{2,1,0:T(2,128)} %param.12) | copy-start | bytes 36868
  83.4 28.0 %all-to-all-start = ((bf16[2048,2,256]{0,2,1:T(8,128)(2,1)}), bf16[2048,2,256]{0,2,1:T(8,128)(2,1)S(1)}, u32[]{:S(2)}, u32[]{:S(2)}) async-start(bf16[2048,2,256]{0,2,1:T(8,128)(2,1)} %bitcast.42), calls=%async_computation | async-start | bytes 4194304 | tf_op jit(solution)/shard_map/all_to_all | solution.py:35
  111.4 5.3 %copy-start.3 = (s32[1,2,1536]{2,1,0:T(2,128)S(1)}, s32[1,2,1536]{2,1,0:T(2,128)}, u32[]{:S(2)}) copy-start(s32[1,2,1536]{2,1,0:T(2,128)} %param.11) | copy-start | bytes 36868
  111.4 5.3 %copy-start.2 = (f32[1,2,1536]{2,1,0:T(2,128)S(1)}, f32[1,2,1536]{2,1,0:T(2,128)}, u32[]{:S(2)}) copy-start(f32[1,2,1536]{2,1,0:T(2,128)} %param.13) | copy-start | bytes 36868
  113.9 48.5 %collective-permute-start = (bf16[4096,256]{1,0:T(8,128)(2,1)}, bf16[4096,256]{1,0:T(8,128)(2,1)}, u32[]{:S(2)}, u32[]{:S(2)}) collective-permute-start(bf16[4096,256]{1,0:T(8,128)(2,1)} %bitcast.6), channel_id=1, source_target_pairs={{0,2},{2,4},{4,6},{6,8},{8,10},{10,12},{12,14},{14,16},{16,18},{18... | collective-permute-start | bytes 6291464 | tf_op jit(solution)/shard_map/ppermute | solution.py:10
  116.7 62.0 %collective-permute-start.1 = (bf16[4096,256]{1,0:T(8,128)(2,1)}, bf16[4096,256]{1,0:T(8,128)(2,1)S(1)}, u32[]{:S(2)}, u32[]{:S(2)}) collective-permute-start(bf16[4096,256]{1,0:T(8,128)(2,1)} %bitcast.6), channel_id=1, source_target_pairs={{0,30},{2,0},{4,2},{6,4},{8,6},{10,8},{12,10},{14,12},{16,14},{18,... | collective-permute-start | bytes 6291464 | tf_op jit(solution)/shard_map/ppermute | solution.py:10
  194.1 2.0 copy-start
  194.1 2.0 copy-start.1
Sparse Core Ops, SparseCore 0:
  10.1 58.6 all-gather.1
where the time goes:
time: 226 us; the launch traced here: 225 us
  waiting for transfers between devices  124 us (55%)
  local copies, waits for them, and re-layouts  34.2 us (15%)
  other arithmetic  32 us (14%)
  matrix products  14.7 us (7%)
  between operations  14.2 us (6%)
  starting transfers between devices  6.68 us (3%)
    all_gather x1, waiting for transfers between devices, on_device(): lax.all_gather(live_block, 'panel', axis=0, tiled=True)  58.8 us
    ppermute x2, waiting for transfers between devices, shifted(): return lax.ppermute(value, axis, pairs)  41.7 us
    all_to_all x1, waiting for transfers between devices, on_device(): lax.all_to_all(settled, 'panel', split_axis=1, concat_axis=0, tiled=True)  23.1 us
    scatter-add x1, other arithmetic, on_device(): result = columns_all.astype(jnp.float32).at[targets].add(-jumps)  22 us
    dot_general x1, matrix products, on_device(): jnp.dot(flex_panel, lax.all_gather(live_block, 'panel', axis=0, tiled=Tru...  14.7 us
    gather x2, local copies, waits for them, and re-layouts, interpolate(): first_rows = arrived[position].astype(jnp.float32)  10.7 us
    gather x2, local copies, waits for them, and re-layouts, interpolate(): second_rows = arrived[position + 1].astype(jnp.float32)  10.7 us
    gather x1, local copies, waits for them, and re-layouts, on_device(): from_lower = lower_all[send_rows[lower_region, 1]]  5.51 us
  transfers between devices with their start and end apart: 4, of which 3 were waited for; matrix products, arithmetic and copies ran while one was open for 9% of the time, Pallas kernels for 0%

commit v1 on v0

--- a/solution.py
+++ b/solution.py
@@ -2,6 +2,19 @@
 import jax.numpy as jnp
 from jax import lax
 from jax.sharding import PartitionSpec as P
+
+
+def lines_serve(xs, lane_axis="panel"):
+    piece_next = lax.axis_index(lane_axis)
+    arr_out = lax.axis_size(lane_axis)
+    odd, side_arr, val = (arr_out, piece_next, xs.shape[0])
+    t1, r1 = (xs, 1)
+    while r1 < odd:
+        small = tuple(((it, (it - r1) % odd) for it in range(odd)))
+        top = lax.ppermute(t1, axis_name=lane_axis, perm=small)
+        t1 = jnp.concatenate([t1, top], axis=0)
+        r1 = 2 * r1
+    return jnp.roll(t1, shift=side_arr * val, axis=0)
 
 
 def shifted(value, axis, steps):
@@ -26,11 +39,7 @@
     row_ids = first_row + jnp.arange(rows_here, dtype=jnp.int32)
     live_here = (row_ids < interface_sizes[0])[:, None]
     live_block = jnp.where(live_here, local_block, jnp.zeros((), local_block.dtype))
-    image = jnp.dot(
-        flex_panel,
-        lax.all_gather(live_block, "panel", axis=0, tiled=True),
-        preferred_element_type=jnp.float32,
-    )
+    image = jnp.dot(flex_panel, lines_serve(live_block), preferred_element_type=jnp.float32)
     settled = jnp.where(live_here, image, jnp.zeros((), image.dtype)).astype(jnp.bfloat16)
     columns_all = lax.all_to_all(settled, "panel", split_axis=1, concat_axis=0, tiled=True)
     region_index = lax.axis_index("region")

time: 226 us -> 207 us (0.916)
  waiting for transfers between devices: 124 us -> 110 us
  between operations: 14.2 us -> 0.86 us
  matrix products: 14.7 us -> 21.9 us
  starting transfers between devices: 6.68 us -> 9.18 us
    all_gather x1 -> x0, waiting for transfers between devices: 58.8 us -> none  [on_device(): lax.all_gather(live_block, 'panel', axis=0, tiled=True)]
    ppermute x0 -> x1, waiting for transfers between devices: none -> 45.4 us  [lines_serve(): top = lax.ppermute(t1, axis_name=lane_axis, perm=small)]
    dot_general x1, matrix products: 14.7 us -> 21.9 us  [on_device(): jnp.dot(flex_panel, lines_serve(live_block), preferred_element_type=jnp.f...]
  transfers between devices with their start and end apart: 4 -> 4, of which waited for: 3 -> 3; matrix products, arithmetic and copies ran while one was open for 9% -> 10% of each run, Pallas kernels for 0% -> 0%
where the time goes in v1:
time: 207 us
  waiting for transfers between devices  110 us (53%)
  local copies, waits for them, and re-layouts  34.2 us (17%)
  other arithmetic  31.1 us (15%)
  matrix products  21.9 us (11%)
  starting transfers between devices  9.18 us (4%)
    ppermute x1, waiting for transfers between devices, lines_serve(): top = lax.ppermute(t1, axis_name=lane_axis, perm=small)  45.4 us
    ppermute x2, waiting for transfers between devices, shifted(): return lax.ppermute(value, axis, pairs)  41.7 us
    all_to_all x1, waiting for transfers between devices, on_device(): lax.all_to_all(settled, 'panel', split_axis=1, concat_axis=0, tiled=True)  22.7 us
    scatter-add x1, other arithmetic, on_device(): result = columns_all.astype(jnp.float32).at[targets].add(-jumps)  22 us
    dot_general x1, matrix products, on_device(): jnp.dot(flex_panel, lines_serve(live_block), preferred_element_type=jnp.f...  21.9 us
    gather x2, local copies, waits for them, and re-layouts, interpolate(): first_rows = arrived[position].astype(jnp.float32)  10.7 us
    gather x2, local copies, waits for them, and re-layouts, interpolate(): second_rows = arrived[position + 1].astype(jnp.float32)  10.7 us
    gather x1, local copies, waits for them, and re-layouts, on_device(): from_lower = lower_all[send_rows[lower_region, 1]]  5.51 us
  transfers between devices with their start and end apart: 4, of which 3 were waited for; matrix products, arithmetic and copies ran while one was open for 10% of the time, Pallas kernels for 0%

profile of v1, /device:TPU:1, one launch (start us, length us, event | category | flops | bytes accessed | tf_op | source)
XLA Modules:
  0.0 207.0 jit_solution(6537777028410654272)
XLA Ops:
  0.7 1.8 bitcast_select_fusion
  2.4 2.1 %collective-permute-start = (bf16[2048,512]{1,0:T(8,128)(2,1)S(1)}, bf16[2048,512]{1,0:T(8,128)(2,1)}, u32[]{:S(2)}, u32[]{:S(2)}) collective-permute-start(bf16[2048,512]{1,0:T(8,128)(2,1)S(1)} %bitcast_select_fusion), channel_id=1, source_target_pairs={{0,1},{1,0},{2,3},{3,2},{4,5},{5,4},{6,7},{7,6},{8,9},{9,8},{10,11... | collective-permute-start | bytes 6291464 | tf_op jit(solution)/shard_map/ppermute | solution.py:14
  4.5 45.4 %collective-permute-done = bf16[2048,512]{1,0:T(8,128)(2,1)} collective-permute-done((bf16[2048,512]{1,0:T(8,128)(2,1)S(1)}, bf16[2048,512]{1,0:T(8,128)(2,1)}, u32[]{:S(2)}, u32[]{:S(2)}) %collective-permute-start) | collective-permute-done | bytes 2097184 | tf_op jit(solution)/shard_map/ppermute | solution.py:14
  50.0 21.9 %select_convert_fusion = bf16[512,2048]{1,0:T(8,128)(2,1)} fusion(bf16[1,2048,4096]{2,1,0:T(8,128)(2,1)} %param.8, s32[]{:T(128)S(6)} %select_n.110, bf16[2048,512]{1,0:T(8,128)(2,1)S(1)} %bitcast_select_fusion, bf16[2048,512]{1,0:T(8,128)(2,1)} %collective-permute-done, pred[2048]{0:T(1024)(128)(4,1)S(1)} %add_compare_fusion), kind=kOutput, calls=%fused_computation.16 | convolution fusion | flops 8608808960 | bytes 23070724 | tf_op jit(solution)/shard_map/dot_general | solution.py:42
  71.9 3.9 %all-to-all-start = ((bf16[2048,2,256]{0,2,1:T(8,128)(2,1)}), bf16[2048,2,256]{0,2,1:T(8,128)(2,1)S(1)}, u32[]{:S(2)}, u32[]{:S(2)}) async-start(bf16[2048,2,256]{0,2,1:T(8,128)(2,1)} %bitcast.41), calls=%async_computation | async-start | bytes 4194304 | tf_op jit(solution)/shard_map/all_to_all | solution.py:44
  75.8 0.0 copy-start.3
  75.8 0.0 copy-start.2
  75.8 0.8 fusion.13
  76.6 0.1 fusion.14
  76.7 22.7 %all-to-all-done = bf16[2048,2,256]{0,2,1:T(8,128)(2,1)S(1)} async-done(((bf16[2048,2,256]{0,2,1:T(8,128)(2,1)}), bf16[2048,2,256]{0,2,1:T(8,128)(2,1)S(1)}, u32[]{:S(2)}, u32[]{:S(2)}) %all-to-all-start) | async-done | bytes 2097184 | tf_op jit(solution)/shard_map/all_to_all | solution.py:44
  99.4 2.5 %copy.9 = bf16[2,2048,256]{2,1,0:T(8,128)(2,1)} copy(bf16[2,2048,256]{1,2,0:T(8,128)(2,1)S(1)} %bitcast.40) | data formatting | bytes 4194304 | tf_op jit(solution)/shard_map/all_to_all | solution.py:44
  101.9 3.2 %collective-permute-start.1 = (bf16[4096,256]{1,0:T(8,128)(2,1)}, bf16[4096,256]{1,0:T(8,128)(2,1)}, u32[]{:S(2)}, u32[]{:S(2)}) collective-permute-start(bf16[4096,256]{1,0:T(8,128)(2,1)} %bitcast.6), channel_id=1, source_target_pairs={{0,2},{2,4},{4,6},{6,8},{8,10},{10,12},{12,14},{14,16},{16,18},{18... | collective-permute-start | bytes 6291464 | tf_op jit(solution)/shard_map/ppermute | solution.py:23
  105.1 0.0 collective-permute-start.2
  105.3 3.9 %bitcast_convert_fusion = f32[4096,256]{1,0:T(8,128)} fusion(bf16[2,2048,256]{2,1,0:T(8,128)(2,1)} %copy.9), kind=kLoop, calls=%fused_computation.54 | loop fusion | flops 1048576 | bytes 6291456 | tf_op jit(solution)/shard_map/convert_element_type | solution.py:57
  109.2 41.7 %collective-permute-done.1 = bf16[4096,256]{1,0:T(8,128)(2,1)} collective-permute-done((bf16[4096,256]{1,0:T(8,128)(2,1)}, bf16[4096,256]{1,0:T(8,128)(2,1)}, u32[]{:S(2)}, u32[]{:S(2)}) %collective-permute-start.1) | collective-permute-done | bytes 2097184 | tf_op jit(solution)/shard_map/ppermute | solution.py:23
  150.9 5.5 %gather_fusion = bf16[1536,256]{1,0:T(8,128)(2,1)S(1)} fusion(bf16[4096,256]{1,0:T(8,128)(2,1)} %collective-permute-done.1, s32[2048]{0:T(1024)S(1)} %pad_clamp_fusion.5), kind=kCustom, calls=%fused_computation | custom fusion | bytes 1579008 | tf_op jit(solution)/shard_map/gather | solution.py:51
  156.4 5.4 %gather_fusion.1 = bf16[1536,256]{1,0:T(8,128)(2,1)} fusion(bf16[1536,256]{1,0:T(8,128)(2,1)S(1)} %gather_fusion, s32[2048]{0:T(1024)S(1)} %get-tuple-element.16), kind=kCustom, calls=%fused_computation.1 | custom fusion | bytes 1579008 | tf_op jit(solution)/shard_map/gather | solution.py:27
  161.8 5.4 %gather_fusion.2 = bf16[1536,256]{1,0:T(8,128)(2,1)} fusion(bf16[1536,256]{1,0:T(8,128)(2,1)S(1)} %gather_fusion, s32[2048]{0:T(1024)S(1)} %get-tuple-element.15), kind=kCustom, calls=%fused_computation.2 | custom fusion | bytes 1579008 | tf_op jit(solution)/shard_map/gather | solution.py:28
  167.1 4.8 %gather_fusion.3 = bf16[1536,256]{1,0:T(8,128)(2,1)S(1)} fusion(bf16[4096,256]{1,0:T(8,128)(2,1)S(1)} %collective-permute-done.2, s32[2048]{0:T(1024)S(1)} %pad_clamp_fusion.2), kind=kCustom, calls=%fused_computation.3 | custom fusion | bytes 1579008 | tf_op jit(solution)/shard_map/gather | solution.py:52
  171.9 5.4 %gather_fusion.4 = bf16[1536,256]{1,0:T(8,128)(2,1)} fusion(bf16[1536,256]{1,0:T(8,128)(2,1)S(1)} %gather_fusion.3, s32[2048]{0:T(1024)S(1)} %get-tuple-element.14), kind=kCustom, calls=%fused_computation.4 | custom fusion | bytes 1579008 | tf_op jit(solution)/shard_map/gather | solution.py:27
  177.2 5.3 %gather_fusion.5 = bf16[1536,256]{1,0:T(8,128)(2,1)} fusion(bf16[1536,256]{1,0:T(8,128)(2,1)S(1)} %gather_fusion.3, s32[2048]{0:T(1024)S(1)} %get-tuple-element.13), kind=kCustom, calls=%fused_computation.5 | custom fusion | bytes 1579008 | tf_op jit(solution)/shard_map/gather | solution.py:28
  182.6 2.0 multiply_add_fusion.1
  184.6 0.5 multiply_add_fusion
  185.0 22.0 %scatter_custom_fusion = f32[4096,256]{1,0:T(8,128)} fusion(f32[4096,256]{1,0:T(8,128)} %bitcast_convert_fusion, s32[3072]{0:T(1024)S(1)} %bitcast.44, f32[1536,256]{1,0:T(8,128)S(1)} %multiply_add_fusion, f32[]{:T(128)} %constant.83, f32[1536,256]{1,0:T(8,128)S(1)} %multiply_add_fusion.1), kind=kCustom, calls=%fused_computation.18 | custom fusion | flops 2359296 | bytes 7340544 | tf_op jit(solution)/shard_map/scatter-add | solution.py:57
  (18 shorter events, 0.1 us)
Async XLA Ops:
  2.4 47.5 %collective-permute-start = (bf16[2048,512]{1,0:T(8,128)(2,1)S(1)}, bf16[2048,512]{1,0:T(8,128)(2,1)}, u32[]{:S(2)}, u32[]{:S(2)}) collective-permute-start(bf16[2048,512]{1,0:T(8,128)(2,1)S(1)} %bitcast_select_fusion), channel_id=1, source_target_pairs={{0,1},{1,0},{2,3},{3,2},{4,5},{5,4},{6,7},{7,6},{8,9},{9,8},{10,11... | collective-permute-start | bytes 6291464 | tf_op jit(solution)/shard_map/ppermute | solution.py:14
  71.9 4.8 %copy-start.4 = (s32[1,2,1536]{2,1,0:T(2,128)S(1)}, s32[1,2,1536]{2,1,0:T(2,128)}, u32[]{:S(2)}) copy-start(s32[1,2,1536]{2,1,0:T(2,128)} %param.12) | copy-start | bytes 36868
  71.9 27.6 %all-to-all-start = ((bf16[2048,2,256]{0,2,1:T(8,128)(2,1)}), bf16[2048,2,256]{0,2,1:T(8,128)(2,1)S(1)}, u32[]{:S(2)}, u32[]{:S(2)}) async-start(bf16[2048,2,256]{0,2,1:T(8,128)(2,1)} %bitcast.41), calls=%async_computation | async-start | bytes 4194304 | tf_op jit(solution)/shard_map/all_to_all | solution.py:44
  75.8 29.4 %copy-start.3 = (s32[1,2,1536]{2,1,0:T(2,128)S(1)}, s32[1,2,1536]{2,1,0:T(2,128)}, u32[]{:S(2)}) copy-start(s32[1,2,1536]{2,1,0:T(2,128)} %param.11) | copy-start | bytes 36868
  75.8 29.4 %copy-start.2 = (f32[1,2,1536]{2,1,0:T(2,128)S(1)}, f32[1,2,1536]{2,1,0:T(2,128)}, u32[]{:S(2)}) copy-start(f32[1,2,1536]{2,1,0:T(2,128)} %param.13) | copy-start | bytes 36868
  101.9 49.0 %collective-permute-start.1 = (bf16[4096,256]{1,0:T(8,128)(2,1)}, bf16[4096,256]{1,0:T(8,128)(2,1)}, u32[]{:S(2)}, u32[]{:S(2)}) collective-permute-start(bf16[4096,256]{1,0:T(8,128)(2,1)} %bitcast.6), channel_id=1, source_target_pairs={{0,2},{2,4},{4,6},{6,8},{8,10},{10,12},{12,14},{14,16},{16,18},{18... | collective-permute-start | bytes 6291464 | tf_op jit(solution)/shard_map/ppermute | solution.py:23
  105.1 62.0 %collective-permute-start.2 = (bf16[4096,256]{1,0:T(8,128)(2,1)}, bf16[4096,256]{1,0:T(8,128)(2,1)S(1)}, u32[]{:S(2)}, u32[]{:S(2)}) collective-permute-start(bf16[4096,256]{1,0:T(8,128)(2,1)} %bitcast.6), channel_id=1, source_target_pairs={{0,30},{2,0},{4,2},{6,4},{8,6},{10,8},{12,10},{14,12},{16,14},{18,... | collective-permute-start | bytes 6291464 | tf_op jit(solution)/shard_map/ppermute | solution.py:23
  182.6 2.0 copy-start
  182.6 2.0 copy-start.1
